TPU v7x, 32 devices: a whole 2x2x4 slice. The times are simulated.
32 devices in a mesh: groups: 2 (over y), seq: 4 (over x, core), heads: 4 (over z).
Axes of the slice: x: 2, y: 2, z: 4, core: 2. Of those that a mesh axis runs over, the one named last changes fastest.
Arguments:
- tokens: bfloat16 [4096, 8192], P(('groups', 'seq'), 'heads'), parts along dimension 0, may hold values from -6 to 6
- xz_weight: bfloat16 [8192, 32768], P(None, ('heads', 'seq')), may hold values from -0.0625 to 0.0625
- bc_weight: bfloat16 [8192, 2048], P(None, 'heads'), may hold values from -0.0625 to 0.0625
- step_weight: bfloat16 [8192, 256], P(None, 'heads'), may hold values from -0.0625 to 0.0625
- step_bias: float32 [256], P('heads'), may hold values from -4 to -2
- decay_log: float32 [256], P('heads'), may hold values from -5.3 to -0.7
- skip_gain: float32 [256], P('heads'), may hold values from 0.5 to 2
- conv_weight: float32 [4, 16384], P(None, 'heads'), may hold values from -3 to 3
- conv_bias: float32 [16384], P('heads'), may hold values from -3 to 3
- bc_conv_weight: float32 [4, 2048], replicated, may hold values from -3 to 3
- bc_conv_bias: float32 [2048], replicated, may hold values from -3 to 3
- norm_gain: float32 [16384], P('heads'), may hold values from 0.1 to 1.9
- step_bounds: int32 [32], P('groups'), parts along dimension 0, may hold values from 0 to 2047, as said below
- readers: int32 [32], P('groups'), parts along dimension 0, may hold values from 0 to 3, as said below
Outputs:
- mixed: bfloat16 [4096, 16384], P(('groups', 'seq'), 'heads'), parts along dimension 0
- handoff: bfloat16 [8, 4, 256, 64, 128], P(('groups', 'heads'), None, 'seq'), parts along dimension 0
There are 2 independent parts, one for each index of `groups`. A program takes and returns all parts, laid end to end along the dimension named above; an argument that names none is the same for every part. Nothing has to cross between parts.
Inputs may be any that keep to these rules, and one draw needn't show every extreme that they name: `step_bounds`: boundary j * 4 + i, for i < 4, lies in section j: positions j * 512 to (j + 1) * 512 - 1. The first boundary is at position 0 and the last at 2047. `readers`: among the 4 boundaries of each section every reader appears exactly once.
All inputs are finite; a program needn't handle non-finite values.
Results may differ from a plain program's by a relative error of at most 0.0056.
Values may be sent and summed in bfloat16 or wider, within the bound.
A program may use at most 384 MiB of HBM per device.

v0:
```python
import jax
import jax.numpy as jnp
from jax import lax
from jax.sharding import PartitionSpec as P

H = 256
P_SIZE = 64
N = 128
G = 8
CH = 256
EPSILON = 1e-05
HIGHEST_PRECISION = lax.Precision.HIGHEST


def from_behind(value, axis, steps):
    count = lax.axis_size(axis)
    first, last = (max(0, -steps), min(count, count - steps))
    return lax.ppermute(value, axis, [(source, source + steps) for source in range(first, last)])


def entering(part, axis, combine, identity):
    place = lax.axis_index(axis)
    gathered = jax.tree.map(lambda a: lax.all_gather(a, axis), part)
    state = jax.tree.map(lambda a, e: jnp.zeros_like(a) + jnp.asarray(e, a.dtype), part, identity)

    def one(step, state):
        return combine(
            state, jax.tree.map(lambda a: lax.dynamic_index_in_dim(a, step, 0, False), gathered)
        )

    return lax.fori_loop(0, place, one, state)


def conv_rows(prefix, raw_rows, kernel, shift_bias):
    row_count = raw_rows.shape[0]
    padded = jnp.concatenate([prefix, raw_rows], axis=0).astype(jnp.float32)
    summed = jnp.broadcast_to(shift_bias[None, :], raw_rows.shape)
    for tap_index in range(kernel.shape[0]):
        summed = summed + kernel[tap_index][None, :] * padded[tap_index : tap_index + row_count]
    return jax.nn.silu(summed).astype(jnp.bfloat16)


def shards(
    tokens,
    xz_weight,
    bc_weight,
    step_weight,
    step_bias,
    decay_log,
    skip_gain,
    conv_weight,
    conv_bias,
    bc_conv_weight,
    bc_conv_bias,
    norm_gain,
    step_bounds,
    readers,
):
    head_devices = lax.axis_size("heads")
    section = lax.axis_index("seq")
    head_block = lax.axis_index("heads")
    local_heads = H // head_devices
    per_group = H // G
    local_groups = max(1, local_heads // per_group)
    group_heads = local_heads // local_groups
    first_group = head_block * local_heads // per_group
    gathered = lax.all_gather(tokens, "heads", axis=1, tiled=True)
    row_count = gathered.shape[0]
    xz_rows = jnp.dot(
        gathered,
        lax.all_gather(xz_weight, "seq", axis=1, tiled=True),
        preferred_element_type=jnp.float32,
    ).astype(jnp.bfloat16)
    head_cols = xz_rows.reshape(row_count, local_heads, 2 * P_SIZE)
    inner_raw = head_cols[:, :, :P_SIZE].reshape(row_count, local_heads * P_SIZE)
    gate_raw = head_cols[:, :, P_SIZE:].reshape(row_count, local_groups, group_heads, P_SIZE)
    bc_part = jnp.dot(gathered, bc_weight, preferred_element_type=jnp.float32).astype(jnp.bfloat16)
    step_raw = jnp.dot(gathered, step_weight, preferred_element_type=jnp.float32)
    bc_every = lax.all_gather(bc_part, "heads", axis=1, tiled=True)
    width_bc = local_groups * 2 * N
    bc_mine = lax.dynamic_slice_in_dim(bc_every, first_group * 2 * N, width_bc, 1)
    kernel_bc = lax.dynamic_slice_in_dim(bc_conv_weight, first_group * 2 * N, width_bc, 1)
    shift_bc = lax.dynamic_slice_in_dim(bc_conv_bias, first_group * 2 * N, width_bc, 0)
    taps = conv_weight.shape[0]
    joined = jnp.concatenate([inner_raw, bc_mine], axis=1)
    previous = from_behind(joined[row_count - taps + 1 :], "seq", 1)
    inner_conv = conv_rows(
        previous[:, : local_heads * P_SIZE], inner_raw, conv_weight, conv_bias
    ).reshape(row_count, local_groups, group_heads, P_SIZE)
    bc_conv = conv_rows(previous[:, local_heads * P_SIZE :], bc_mine, kernel_bc, shift_bc).reshape(
        row_count, local_groups, 2 * N
    )
    b_input = bc_conv[:, :, :N]
    c_input = bc_conv[:, :, N:]
    step_size = jax.nn.softplus(step_raw + step_bias[None, :]).reshape(
        row_count, local_groups, group_heads
    )
    decay_rate = -jnp.exp(decay_log).reshape(local_groups, group_heads)[None] * step_size
    blocks = row_count // CH
    causal = lax.broadcasted_iota(jnp.int32, (CH, CH), 0) >= lax.broadcasted_iota(
        jnp.int32, (CH, CH), 1
    )
    running = jnp.zeros((local_groups, group_heads, P_SIZE, N), jnp.float32)
    local_starts = []
    intra_parts = []
    cum_parts = []
    block_totals = []
    for block_index in range(blocks):
        first_row = block_index * CH
        inner_blk = inner_conv[first_row : first_row + CH]
        b_blk = b_input[first_row : first_row + CH]
        c_blk = c_input[first_row : first_row + CH]
        step_blk = step_size[first_row : first_row + CH]
        cum_block = jnp.cumsum(decay_rate[first_row : first_row + CH], axis=0)
        scores = jnp.einsum("tgn,sgn->gts", c_blk, b_blk, preferred_element_type=jnp.float32)
        cum_gap = cum_block[:, None] - cum_block[None, :]
        weight = (
            jnp.where(causal[:, :, None, None], jnp.exp(jnp.minimum(cum_gap, 0.0)), 0.0)
            * step_blk[None]
        )
        mixing = (weight * jnp.transpose(scores, (1, 2, 0))[:, :, :, None]).astype(jnp.bfloat16)
        intra_parts.append(
            jnp.einsum("tsgr,sgrp->tgrp", mixing, inner_blk, preferred_element_type=jnp.float32)
        )
        cum_parts.append(cum_block)
        local_starts.append(running)
        block_total = cum_block[-1]
        block_totals.append(block_total)
        carry_weight = jnp.exp(block_total[None] - cum_block) * step_blk
        weighted = (inner_blk.astype(jnp.float32) * carry_weight[..., None]).astype(jnp.bfloat16)
        running = jnp.exp(block_total)[..., None, None] * running + jnp.einsum(
            "sgrp,sgn->grpn", weighted, b_blk, preferred_element_type=jnp.float32
        )
    section_decay = block_totals[0]
    block_index = 1
    section_decay = section_decay + block_totals[block_index]

    def combine(earlier, later):
        return (earlier[0] + later[0], jnp.exp(later[0])[..., None, None] * earlier[1] + later[1])

    identity = (jnp.zeros_like(section_decay), jnp.zeros_like(running))
    incoming = entering((section_decay, running), "seq", combine, identity)[1]
    global_starts = []
    ssd_parts = []
    prior_decay = jnp.zeros_like(section_decay)
    for block_index in range(blocks):
        start_state = local_starts[block_index] + jnp.exp(prior_decay)[..., None, None] * incoming
        global_starts.append(start_state)
        prior_decay = prior_decay + block_totals[block_index]
        first_row = block_index * CH
        c_blk = c_input[first_row : first_row + CH]
        outer_part = jnp.exp(cum_parts[block_index])[..., None] * jnp.einsum(
            "tgn,grpn->tgrp", c_blk.astype(jnp.float32), start_state, precision=HIGHEST_PRECISION
        )
        ssd_parts.append(intra_parts[block_index] + outer_part)
    ssd = jnp.concatenate(ssd_parts, axis=0) + skip_gain.reshape(local_groups, group_heads)[
        None, :, :, None
    ] * inner_conv.astype(jnp.float32)
    gated = ssd * jax.nn.silu(gate_raw.astype(jnp.float32))
    local_square = jnp.sum(gated * gated, axis=(2, 3))
    placed = lax.dynamic_update_slice_in_dim(
        jnp.zeros((row_count, G), jnp.float32), local_square, first_group, 1
    )
    square_total = lax.psum(placed, "heads")
    square_mean = lax.dynamic_slice_in_dim(square_total, first_group, local_groups, 1) / (
        per_group * P_SIZE
    )
    normed = (
        gated
        * lax.rsqrt(square_mean + EPSILON)[:, :, None, None]
        * norm_gain.reshape(local_groups, group_heads, P_SIZE)[None]
    )
    mixed = normed.astype(jnp.bfloat16).reshape(row_count, local_heads * P_SIZE)
    cum_all = jnp.concatenate(cum_parts, axis=0)
    starts_all = jnp.stack(global_starts, axis=0)
    positions = lax.broadcasted_iota(jnp.int32, (row_count,), 0)
    bound_local = (
        lax.dynamic_slice_in_dim(step_bounds, section * head_devices, head_devices, 0)
        - section * row_count
    )
    reader_local = lax.dynamic_slice_in_dim(readers, section * head_devices, head_devices, 0)
    block_of = bound_local // CH
    cum_at = cum_all[bound_local]
    inside_mask = (positions[None, :] // CH == block_of[:, None]) & (
        positions[None, :] <= bound_local[:, None]
    )
    cum_gap = cum_at[:, None] - cum_all[None]
    bound_weight = (
        jnp.where(inside_mask[:, :, None, None], jnp.exp(jnp.minimum(cum_gap, 0.0)), 0.0)
        * step_size[None]
    )
    bound_weighted = (inner_conv[None].astype(jnp.float32) * bound_weight[..., None]).astype(
        jnp.bfloat16
    )
    inside = jnp.einsum(
        "bsgrp,sgn->bgrpn", bound_weighted, b_input, preferred_element_type=jnp.float32
    )
    states = jnp.exp(cum_at)[..., None, None] * starts_all[block_of] + inside
    inverse = jnp.argsort(reader_local)
    ordered = states[inverse].reshape(head_devices, local_heads, P_SIZE, N).astype(jnp.bfloat16)
    arrived = lax.all_to_all(
        lax.all_to_all(ordered, "heads", split_axis=0, concat_axis=1, tiled=True),
        "seq",
        split_axis=1,
        concat_axis=0,
        tiled=True,
    )
    return (mixed, arrived[None])


def solution(mesh):
    in_specs = (
        P(("groups", "seq"), "heads"),
        P(None, ("heads", "seq")),
        P(None, "heads"),
        P(None, "heads"),
        P("heads"),
        P("heads"),
        P("heads"),
        P(None, "heads"),
        P("heads"),
        P(),
        P(),
        P("heads"),
        P("groups"),
        P("groups"),
    )
    out_specs = (P(("groups", "seq"), "heads"), P(("groups", "heads"), None, "seq", None, None))
    return jax.shard_map(shards, mesh=mesh, in_specs=in_specs, out_specs=out_specs, check_vma=False)
```

profile of v0, /device:TPU:6, one launch (start us, length us, event | category | flops | bytes accessed | tf_op | source)
XLA Modules:
  0.0 1422.9 jit_solution(13541814008040680989)
XLA Ops:
  8.0 152.5 %all-gather.6.cloned.1.call-done = bf16[512,8192]{1,0:T(8,128)(2,1)} async-done(((bf16[512,2048]{1,0:T(8,128)(2,1)}), bf16[512,8192]{1,0:T(8,128)(2,1)}) %all-gather.6.cloned.1.call-update) | async-done | bytes 8388624 | tf_op jit(solution)/shard_map/all_gather | solution.py:67
  160.4 11.0 convolution_convert_fusion.1
  174.6 6.4 compare_select_fusion
  185.7 30.3 %all-gather.10.cloned.1.call-done = bf16[512,2048]{1,0:T(8,128)(2,1)} async-done(((bf16[512,512]{1,0:T(8,128)(2,1)}), bf16[512,2048]{1,0:T(8,128)(2,1)}) %all-gather.10.cloned.1.call-update) | async-done | bytes 2097168 | tf_op jit(solution)/shard_map/all_gather | solution.py:79
  217.0 773.3 %all-gather.8.cloned.1.call-done = bf16[8192,8192]{1,0:T(8,128)(2,1)} async-done(((bf16[8192,2048]{1,0:T(8,128)(2,1)}), bf16[8192,8192]{1,0:T(8,128)(2,1)}) %all-gather.8.cloned.1.call-update) | async-done | bytes 134217744 | tf_op jit(solution)/shard_map/all_gather | solution.py:71
  990.3 79.7 %convolution_convert_fusion = bf16[512,8192]{1,0:T(8,128)(2,1)} fusion(bf16[512,8192]{1,0:T(8,128)(2,1)} %all-gather.6.cloned.1.call-done, bf16[8192,8192]{1,0:T(8,128)(2,1)} %all-gather.8.cloned.1.call-done), kind=kOutput, calls=%fused_computation.11 | convolution fusion | flops 68723671040 | bytes 150994944 | tf_op jit(solution)/shard_map/dot_general | solution.py:69
  1070.1 12.0 copy.125
  1082.1 7.6 slice_convert_fusion
  1089.6 6.3 copy.101
  1108.6 10.7 multiply_convert_fusion.6
  1127.3 5.1 all_gather.22
  1134.6 48.9 %all-gather.12.cloned.1.call-done = f32[8,32,64,128]{3,2,1,0:T(8,128)} async-done(((f32[2,32,64,128]{3,2,1,0:T(8,128)}), f32[8,32,64,128]{3,2,1,0:T(8,128)}) %all-gather.12.cloned.1.call-update) | async-done | bytes 8388624 | tf_op jit(solution)/shard_map/all_gather | solution.py:23
  1190.0 5.5 fusion.42
  1201.6 6.8 gather_fusion.1
  1208.5 7.2 fusion.31
  1215.8 6.8 fusion.32
  1222.7 14.6 %fusion.15 = (f32[512,2]{0,1:T(2,128)S(1)}, f32[512,4096]{0,1:T(8,128)}) fusion(f32[256,2,32,64]{0,3,2,1:T(8,128)S(1)} %fusion.31, f32[256,2,32,64]{0,3,2,1:T(8,128)} %fusion.32, f32[512,2,32,64]{0,3,2,1:T(8,128)} %bitcast.150, f32[2,32]{1,0:T(2,128)S(1)} %mul.366, f32[515,4096]{0,1:T(8,128)S(1)} %bitcast.147, f32[4096]{0:T(1024)S(1)} %bitcast.176, ...), kind=kLoop, calls=%fused_computation.30 | loop fusion | flops 50330624 | bytes 58806528 | tf_op jit(solution)/shard_map/reduce_sum | solution.py:160
  1237.3 9.6 bitcast_add_fusion.1
  1247.0 5.3 gather_fusion.2
  1252.3 99.6 %all_to_all.24 = bf16[4,64,64,128]{3,2,1,0:T(8,128)(2,1)} all-to-all(bf16[4,64,64,128]{3,2,1,0:T(8,128)(2,1)} %bitcast.155), channel_id=1, replica_groups=mesh['groups'=2,'seq'=4,'heads'=4] {'heads'}, dimensions={0} | all-to-all | bytes 8388608 | tf_op jit(solution)/shard_map/all_to_all | solution.py:202
  1357.0 17.2 %psum.7 = f32[512,8]{0,1:T(8,128)S(1)} all-reduce(f32[512,8]{0,1:T(8,128)S(1)} %dynamic_update_slice.3), channel_id=1, replica_groups=mesh['groups'=2,'seq'=4,'heads'=4] {'heads'}, use_global_device_ids=true, to_apply=%region_7.8 | all-reduce | flops 4096 | bytes 32768 | tf_op jit(solution)/shard_map/psum | solution.py:164
  1374.3 30.4 %fusion.12 = bf16[512,4096]{0,1:T(8,128)(2,1)} fusion(f32[256,4096]{0,1:T(8,128)} %bitcast.156, f32[256,4096]{0,1:T(8,128)} %bitcast.157, f32[512,64,64]{0,2,1:T(8,128)} %get-tuple-element.76, f32[4096]{0:T(1024)S(1)} %copy-done.29, f32[512,2]{0,1:T(2,128)S(1)} %add_rsqrt_fusion, f32[4096]{0:T(1024)S(1)} %mul.368, f32[515,4096]{0,1:T(8,128)} %copy-done.2, ...), kind=kLoop, calls=%fused_computation.26 | loop fusion | flops 52428800 | bytes 54644736 | tf_op jit(solution)/shard_map/convert_element_type | solution.py:173
  1404.6 6.3 copy.119
  1411.0 5.2 copy.181
  (168 shorter events, 53.7 us)
Async XLA Ops:
  7.2 167.3 %copy-start = (bf16[8192,64]{0,1:T(8,128)(2,1)S(1)}, bf16[8192,64]{0,1:T(8,128)(2,1)}, u32[]{:S(2)}) copy-start(bf16[8192,64]{0,1:T(8,128)(2,1)} %param.19) | copy-start | bytes 3145732
  7.2 153.3 %all-gather.6.cloned.1.call-start = ((), (), s32[]{:S(2)}) async-start(), calls=%async_computation.2 | async-start | bytes 10485760 | tf_op jit(solution)/shard_map/all_gather | solution.py:67
  7.9 208.0 %all-gather.10.cloned.1.call-start = ((), (), s32[]{:S(2)}) async-start(), calls=%async_computation.4 | async-start | bytes 2621440 | tf_op jit(solution)/shard_map/all_gather | solution.py:79
  171.5 818.8 %all-gather.8.cloned.1.call-start = ((), (), s32[]{:S(2)}) async-start(), calls=%async_computation.3 | async-start | bytes 167772160 | tf_op jit(solution)/shard_map/all_gather | solution.py:71
  172.3 1011.3 %all-gather.12.cloned.1.call-start = ((), (), s32[]{:S(2)}) async-start(), calls=%async_computation.5 | async-start | bytes 10485760 | tf_op jit(solution)/shard_map/all_gather | solution.py:23
  174.5 934.0 %copy-start.16 = (f32[1,4096]{1,0:T(1,128)}, f32[1,4096]{1,0:T(1,128)S(1)}, u32[]{:S(2)}) copy-start(f32[1,4096]{1,0:T(1,128)S(1)} %get-tuple-element.96) | copy-start | bytes 49156
  174.5 934.0 %copy-start.18 = (f32[1,4096]{1,0:T(1,128)}, f32[1,4096]{1,0:T(1,128)S(1)}, u32[]{:S(2)}) copy-start(f32[1,4096]{1,0:T(1,128)S(1)} %get-tuple-element.97) | copy-start | bytes 49156
  174.5 934.0 %copy-start.20 = (f32[1,4096]{1,0:T(1,128)}, f32[1,4096]{1,0:T(1,128)S(1)}, u32[]{:S(2)}) copy-start(f32[1,4096]{1,0:T(1,128)S(1)} %get-tuple-element.98) | copy-start | bytes 49156
  184.2 885.8 %copy-start.12 = (f32[256,64]{0,1:T(8,128)}, f32[256,64]{0,1:T(8,128)S(1)}, u32[]{:S(2)}) copy-start(f32[256,64]{0,1:T(8,128)S(1)} %get-tuple-element.85) | copy-start | bytes 196612
  184.3 885.8 %copy-start.14 = (f32[256,64]{0,1:T(8,128)}, f32[256,64]{0,1:T(8,128)S(1)}, u32[]{:S(2)}) copy-start(f32[256,64]{0,1:T(8,128)S(1)} %get-tuple-element.84) | copy-start | bytes 196612
  1096.8 5.3 collective-permute-start
  1100.1 21.6 %copy-start.27 = (f32[2,32]{1,0:T(2,128)}, f32[2,32]{1,0:T(2,128)S(1)}, u32[]{:S(2)}) copy-start(f32[2,32]{1,0:T(2,128)S(1)} %get-tuple-element.104) | copy-start | bytes 772
  1103.1 29.5 %copy-start.10 = (bf16[512,2,256]{2,1,0:T(2,128)(2,1)}, bf16[512,2,256]{2,1,0:T(2,128)(2,1)S(1)}, u32[]{:S(2)}) copy-start(bf16[512,2,256]{2,1,0:T(2,128)(2,1)S(1)} %reshape.225) | copy-start | bytes 1572868
  1108.5 10.8 copy-start.2
  1208.5 7.2 copy-start.6
  1208.5 7.2 copy-start.9
  1208.5 7.2 copy-start.11
  1208.5 7.2 copy-start.13
  1208.5 7.2 copy-start.25
  1215.7 7.0 copy-start.4
  1222.7 14.6 %slice-start.3 = ((bf16[512,2,256]{2,1,0:T(2,128)(2,1)}), bf16[512,2,128]{2,1,0:T(2,128)(2,1)S(1)}, s32[]{:S(2)}) async-start(bf16[512,2,256]{2,1,0:T(2,128)(2,1)} %copy-done.10), calls=%async_computation.9 | async-start | bytes 524288 | tf_op jit(solution)/shard_map/slice | solution.py:93
  1252.3 121.9 %copy-start.29 = (f32[4096]{0:T(1024)S(1)}, f32[4096]{0:T(1024)}, u32[]{:S(2)}) copy-start(f32[4096]{0:T(1024)} %param.27) | copy-start | bytes 49156
  1351.9 59.1 %all-to-all-start.1 = ((bf16[1,256,64,128]{3,2,0,1:T(8,128)(2,1)}), bf16[1,256,64,128]{3,2,0,1:T(8,128)(2,1)}, u32[]{:S(2)}, u32[]{:S(2)}) async-start(bf16[1,256,64,128]{3,2,0,1:T(8,128)(2,1)} %bitcast.154), calls=%async_computation.1 | async-start | bytes 8388608 | tf_op jit(solution)/shard_map/all_to_all | solution.py:201
  1374.2 41.9 %copy-start.1 = (bf16[8192,64]{0,1:T(8,128)(2,1)S(1)}, bf16[8192,64]{0,1:T(8,128)(2,1)}, u32[]{:S(2)}) copy-start(bf16[8192,64]{0,1:T(8,128)(2,1)} %param.19) | copy-start | bytes 3145732
  (22 other events, 111.7 us)
Sparse Core Ops, SparseCore 0:
  9.6 150.8 all-gather.5
  171.6 44.2 all-gather.9
  217.5 772.7 all-gather.7
  1125.2 58.2 all-gather.11
where the time goes:
time: 1430 us; the launch traced here: 1420 us
  waiting for transfers between devices  1010 us (71%)
  matrix products  135 us (9%)
  blocking collectives  122 us (9%)
  other arithmetic  83.8 us (6%)
  local copies, waits for them, and re-layouts  50.9 us (4%)
  between operations  14.8 us (1%)
    all_gather x1, waiting for transfers between devices, shards(): lax.all_gather(xz_weight, 'seq', axis=1, tiled=True)  773 us
    all_gather x1, waiting for transfers between devices, shards(): gathered = lax.all_gather(tokens, 'heads', axis=1, tiled=True)  152 us
    all_to_all x1, blocking collectives, shards(): lax.all_to_all(ordered, 'heads', split_axis=0, concat_axis=1, tiled=True)  99.6 us
    dot_general x1, matrix products, shards(): jnp.dot(gathered, lax.all_gather(xz_weight, 'seq', axis=1, tiled=True), p...  79.7 us
    all_gather x1, waiting for transfers between devices, entering(): gathered = jax.tree.map(lambda a: lax.all_gather(a, axis), part)  48.9 us
    convert_element_type x1, other arithmetic, shards(): mixed = normed.astype(jnp.bfloat16).reshape(row_count, local_heads * P_SIZE)  30.4 us
    all_gather x1, waiting for transfers between devices, shards(): bc_every = lax.all_gather(bc_part, 'heads', axis=1, tiled=True)  30.3 us
  transfers between devices with their start and end apart: 6, of which 5 were waited for; matrix products, arithmetic and copies ran while one was open for 4% of the time, Pallas kernels for 0%

commit v1 on v0

--- a/solution.py
+++ b/solution.py
@@ -10,6 +10,28 @@
 CH = 256
 EPSILON = 1e-05
 HIGHEST_PRECISION = lax.Precision.HIGHEST
+
+
+def joined_along(pieces, dim):
+    pieces = jnp.moveaxis(pieces, 0, dim)
+    shape = pieces.shape
+    return pieces.reshape(*shape[:dim], shape[dim] * shape[dim + 1], *shape[dim + 2 :])
+
+
+def ring_gather(value, axis, dim):
+    length = lax.axis_size(axis)
+    pairs = [(i, (i + 1) % length) for i in range(length)]
+    back = [(b, a) for a, b in pairs]
+    lower, upper = ([], [])
+    for step in range(length - 1):
+        if step % 2 == 0:
+            lower.append(lax.ppermute(lower[-1] if lower else value, axis, pairs))
+        else:
+            upper.append(lax.ppermute(upper[-1] if upper else value, axis, back))
+    blocks = jnp.stack([*lower[::-1], value, *upper])
+    shift = lax.axis_index(axis) - len(lower)
+    blocks = blocks[(jnp.arange(length) - shift) % length]
+    return joined_along(blocks, dim)
 
 
 def from_behind(value, axis, steps):
@@ -67,9 +89,7 @@
     gathered = lax.all_gather(tokens, "heads", axis=1, tiled=True)
     row_count = gathered.shape[0]
     xz_rows = jnp.dot(
-        gathered,
-        lax.all_gather(xz_weight, "seq", axis=1, tiled=True),
-        preferred_element_type=jnp.float32,
+        gathered, ring_gather(xz_weight, "seq", 1), preferred_element_type=jnp.float32
     ).astype(jnp.bfloat16)
     head_cols = xz_rows.reshape(row_count, local_heads, 2 * P_SIZE)
     inner_raw = head_cols[:, :, :P_SIZE].reshape(row_count, local_heads * P_SIZE)

time: 1430 us -> 2440 us (1.71)
  local copies, waits for them, and re-layouts: 50.9 us -> 866 us
  other arithmetic: 83.8 us -> 175 us
  waiting for transfers between devices: 1010 us -> 1100 us
    ppermute x0 -> x3, waiting for transfers between devices: none -> 874 us  [the longest x2 874 us: ring_gather(): lower.append(lax.ppermute(lower[-1] if lower else value, axis, pairs))]
    all_gather x1 -> x0, waiting for transfers between devices: 773 us -> none  [shards(): lax.all_gather(xz_weight, 'seq', axis=1, tiled=True)]
    gather x0 -> x257, local copies, waits for them, and re-layouts: none -> 644 us
    unnamed x81 -> x161, local copies, waits for them, and re-layouts: 14.2 us -> 191 us
    another operation x6 -> x7, other arithmetic: 2.58 us -> 90.4 us  [the longest x1 87.3 us: ring_gather(): blocks = jnp.stack([*lower[::-1], value, *upper])]
  transfers between devices with their start and end apart: 6 -> 8, of which waited for: 5 -> 6; matrix products, arithmetic and copies ran while one was open for 4% -> 3% of each run, Pallas kernels for 0% -> 0%
where the time goes in v1:
time: 2440 us; the launch traced here: 2430 us
  waiting for transfers between devices  1100 us (45%)
  local copies, waits for them, and re-layouts  866 us (35%)
  other arithmetic  175 us (7%)
  matrix products  138 us (6%)
  blocking collectives  121 us (5%)
    ppermute x2, waiting for transfers between devices, ring_gather(): lower.append(lax.ppermute(lower[-1] if lower else value, axis, pairs))  874 us
    gather x256, local copies, waits for them, and re-layouts  559 us
    unnamed x161, local copies, waits for them, and re-layouts  191 us
    all_gather x1, waiting for transfers between devices, shards(): gathered = lax.all_gather(tokens, 'heads', axis=1, tiled=True)  151 us
    all_to_all x1, blocking collectives, shards(): lax.all_to_all(ordered, 'heads', split_axis=0, concat_axis=1, tiled=True)  99.2 us
    another operation x1, other arithmetic, ring_gather(): blocks = jnp.stack([*lower[::-1], value, *upper])  87.3 us
    gather x1, local copies, waits for them, and re-layouts, ring_gather(): blocks = blocks[(jnp.arange(length) - shift) % length]  85 us
    dot_general x1, matrix products, shards(): jnp.dot(gathered, ring_gather(xz_weight, 'seq', 1), preferred_element_typ...  80.2 us
  transfers between devices with their start and end apart: 8, of which 6 were waited for; matrix products, arithmetic and copies ran while one was open for 3% of the time, Pallas kernels for 0%

profile of v1, /device:TPU:6, one launch (start us, length us, event | category | flops | bytes accessed | tf_op | source)
XLA Modules:
  0.0 2425.5 jit_solution(13867983308899697824)
XLA Ops:
  9.0 719.8 %collective-permute-done = bf16[8192,2048]{1,0:T(8,128)(2,1)} collective-permute-done((bf16[8192,2048]{1,0:T(8,128)(2,1)}, bf16[8192,2048]{1,0:T(8,128)(2,1)}, u32[]{:S(2)}, u32[]{:S(2)}) %collective-permute-start) | collective-permute-done | bytes 33554464 | tf_op jit(solution)/shard_map/ppermute | solution.py:28
  729.0 151.2 %all-gather.5.cloned.1.call-done = bf16[512,8192]{1,0:T(8,128)(2,1)} async-done(((bf16[512,2048]{1,0:T(8,128)(2,1)}), bf16[512,8192]{1,0:T(8,128)(2,1)}) %all-gather.5.cloned.1.call-update) | async-done | bytes 8388624 | tf_op jit(solution)/shard_map/all_gather | solution.py:89
  937.4 154.3 %collective-permute-done.1 = bf16[8192,2048]{1,0:T(8,128)(2,1)} collective-permute-done((bf16[8192,2048]{1,0:T(8,128)(2,1)}, bf16[8192,2048]{1,0:T(8,128)(2,1)}, u32[]{:S(2)}, u32[]{:S(2)}) %collective-permute-start.1) | collective-permute-done | bytes 33554464 | tf_op jit(solution)/shard_map/ppermute | solution.py:28
  1091.7 87.3 %pad_maximum_fusion = bf16[4,8192,2048]{2,1,0:T(8,128)(2,1)} fusion(bf16[1,8192,2048]{2,1,0:T(8,128)(2,1)} %bitcast.6, bf16[1,8192,2048]{2,1,0:T(8,128)(2,1)} %bitcast.210, bf16[1,8192,2048]{2,1,0:T(8,128)(2,1)} %bitcast.4, bf16[1,8192,2048]{2,1,0:T(8,128)(2,1)} %bitcast.3), kind=kLoop, calls=%fused_computation.53 | loop fusion | flops 201326592 | bytes 268435456 | tf_op jit(solution)/shard_map/stack | solution.py:31
  1179.1 85.0 %fusion.65 = (bf16[4,512,2048]{2,1,0:T(8,128)(2,1)}, bf16[4,512,2048]{2,1,0:T(8,128)(2,1)}, bf16[4,512,2048]{2,1,0:T(8,128)(2,1)}, bf16[4,512,2048]{2,1,0:T(8,12...) fusion(bf16[4,8192,2048]{2,1,0:T(8,128)(2,1)} %pad_maximum_fusion), kind=kLoop, calls=%fused_computation.213 | loop fusion | bytes 268435456 | tf_op jit(solution)/shard_map/gather | solution.py:33
  1268.1 35.2 %while.29 = (s32[]{:T(128)}, bf16[4,512,2048]{2,1,0:T(8,128)(2,1)}, s32[4,1]{0,1:T(1,128)S(1)}, bf16[4,512,2048]{1,2,0:T(8,128)(2,1)}, s32[]{:T(128)}) while((s32[]{:T(128)}, bf16[4,512,2048]{2,1,0:T(8,128)(2,1)}, s32[4,1]{0,1:T(1,128)S(1)}, bf16[4,512,2048]{1,2,0:T(8,128)(2,1)}, s32[]{:T(128)}) %tuple.303), condition=%wide.while_cond, body=%wide.while_body.sunk | while | flops 2 | bytes 12583501 | solution.py:33
  1314.4 35.0 %while.30 = (s32[]{:T(128)}, bf16[4,512,2048]{2,1,0:T(8,128)(2,1)}, s32[4,1]{0,1:T(1,128)S(1)}, bf16[4,512,2048]{1,2,0:T(8,128)(2,1)}, s32[]{:T(128)}) while((s32[]{:T(128)}, bf16[4,512,2048]{2,1,0:T(8,128)(2,1)}, s32[4,1]{0,1:T(1,128)S(1)}, bf16[4,512,2048]{1,2,0:T(8,128)(2,1)}, s32[]{:T(128)}) %tuple.304), condition=%wide.while_cond.1, body=%wide.while_body.1.sunk | while | flops 2 | bytes 12583501 | solution.py:33
  1353.3 34.9 %while.31 = (s32[]{:T(128)}, bf16[4,512,2048]{2,1,0:T(8,128)(2,1)}, s32[4,1]{0,1:T(1,128)S(1)}, bf16[4,512,2048]{1,2,0:T(8,128)(2,1)}, s32[]{:T(128)}) while((s32[]{:T(128)}, bf16[4,512,2048]{2,1,0:T(8,128)(2,1)}, s32[4,1]{0,1:T(1,128)S(1)}, bf16[4,512,2048]{1,2,0:T(8,128)(2,1)}, s32[]{:T(128)}) %tuple.305), condition=%wide.while_cond.2, body=%wide.while_body.2.sunk | while | flops 2 | bytes 12583501 | solution.py:33
  1392.1 34.9 %while.32 = (s32[]{:T(128)}, bf16[4,512,2048]{2,1,0:T(8,128)(2,1)}, s32[4,1]{0,1:T(1,128)S(1)}, bf16[4,512,2048]{1,2,0:T(8,128)(2,1)}, s32[]{:T(128)}) while((s32[]{:T(128)}, bf16[4,512,2048]{2,1,0:T(8,128)(2,1)}, s32[4,1]{0,1:T(1,128)S(1)}, bf16[4,512,2048]{1,2,0:T(8,128)(2,1)}, s32[]{:T(128)}) %tuple.306), condition=%wide.while_cond.3, body=%wide.while_body.3.sunk | while | flops 2 | bytes 12583501 | solution.py:33
  1430.9 34.9 %while.33 = (s32[]{:T(128)}, bf16[4,512,2048]{2,1,0:T(8,128)(2,1)}, s32[4,1]{0,1:T(1,128)S(1)}, bf16[4,512,2048]{1,2,0:T(8,128)(2,1)}, s32[]{:T(128)}) while((s32[]{:T(128)}, bf16[4,512,2048]{2,1,0:T(8,128)(2,1)}, s32[4,1]{0,1:T(1,128)S(1)}, bf16[4,512,2048]{1,2,0:T(8,128)(2,1)}, s32[]{:T(128)}) %tuple.307), condition=%wide.while_cond.4, body=%wide.while_body.4.sunk | while | flops 2 | bytes 12583501 | solution.py:33
  1469.8 35.0 %while.34 = (s32[]{:T(128)}, bf16[4,512,2048]{2,1,0:T(8,128)(2,1)}, s32[4,1]{0,1:T(1,128)S(1)}, bf16[4,512,2048]{1,2,0:T(8,128)(2,1)}, s32[]{:T(128)}) while((s32[]{:T(128)}, bf16[4,512,2048]{2,1,0:T(8,128)(2,1)}, s32[4,1]{0,1:T(1,128)S(1)}, bf16[4,512,2048]{1,2,0:T(8,128)(2,1)}, s32[]{:T(128)}) %tuple.308), condition=%wide.while_cond.5, body=%wide.while_body.5.sunk | while | flops 2 | bytes 12583501 | solution.py:33
  1508.8 35.1 %while.35 = (s32[]{:T(128)}, bf16[4,512,2048]{2,1,0:T(8,128)(2,1)}, s32[4,1]{0,1:T(1,128)S(1)}, bf16[4,512,2048]{1,2,0:T(8,128)(2,1)}, s32[]{:T(128)}) while((s32[]{:T(128)}, bf16[4,512,2048]{2,1,0:T(8,128)(2,1)}, s32[4,1]{0,1:T(1,128)S(1)}, bf16[4,512,2048]{1,2,0:T(8,128)(2,1)}, s32[]{:T(128)}) %tuple.309), condition=%wide.while_cond.6, body=%wide.while_body.6.sunk | while | flops 2 | bytes 12583501 | solution.py:33
  1547.9 35.0 %while.36 = (s32[]{:T(128)}, bf16[4,512,2048]{2,1,0:T(8,128)(2,1)}, s32[4,1]{0,1:T(1,128)S(1)}, bf16[4,512,2048]{1,2,0:T(8,128)(2,1)}, s32[]{:T(128)}) while((s32[]{:T(128)}, bf16[4,512,2048]{2,1,0:T(8,128)(2,1)}, s32[4,1]{0,1:T(1,128)S(1)}, bf16[4,512,2048]{1,2,0:T(8,128)(2,1)}, s32[]{:T(128)}) %tuple.310), condition=%wide.while_cond.7, body=%wide.while_body.7.sunk | while | flops 2 | bytes 12583501 | solution.py:33
  1587.0 35.0 %while.37 = (s32[]{:T(128)}, bf16[4,512,2048]{2,1,0:T(8,128)(2,1)}, s32[4,1]{0,1:T(1,128)S(1)}, bf16[4,512,2048]{1,2,0:T(8,128)(2,1)}, s32[]{:T(128)}) while((s32[]{:T(128)}, bf16[4,512,2048]{2,1,0:T(8,128)(2,1)}, s32[4,1]{0,1:T(1,128)S(1)}, bf16[4,512,2048]{1,2,0:T(8,128)(2,1)}, s32[]{:T(128)}) %tuple.311), condition=%wide.while_cond.8, body=%wide.while_body.8.sunk | while | flops 2 | bytes 12583501 | solution.py:33
  1625.9 34.9 %while.38 = (s32[]{:T(128)}, bf16[4,512,2048]{2,1,0:T(8,128)(2,1)}, s32[4,1]{0,1:T(1,128)S(1)}, bf16[4,512,2048]{1,2,0:T(8,128)(2,1)}, s32[]{:T(128)}) while((s32[]{:T(128)}, bf16[4,512,2048]{2,1,0:T(8,128)(2,1)}, s32[4,1]{0,1:T(1,128)S(1)}, bf16[4,512,2048]{1,2,0:T(8,128)(2,1)}, s32[]{:T(128)}) %tuple.312), condition=%wide.while_cond.9, body=%wide.while_body.9.sunk | while | flops 2 | bytes 12583501 | solution.py:33
  1664.7 34.9 %while.39 = (s32[]{:T(128)}, bf16[4,512,2048]{2,1,0:T(8,128)(2,1)}, s32[4,1]{0,1:T(1,128)S(1)}, bf16[4,512,2048]{1,2,0:T(8,128)(2,1)}, s32[]{:T(128)}) while((s32[]{:T(128)}, bf16[4,512,2048]{2,1,0:T(8,128)(2,1)}, s32[4,1]{0,1:T(1,128)S(1)}, bf16[4,512,2048]{1,2,0:T(8,128)(2,1)}, s32[]{:T(128)}) %tuple.313), condition=%wide.while_cond.10, body=%wide.while_body.10.sunk | while | flops 2 | bytes 12583501 | solution.py:33
  1703.5 34.9 %while.40 = (s32[]{:T(128)}, bf16[4,512,2048]{2,1,0:T(8,128)(2,1)}, s32[4,1]{0,1:T(1,128)S(1)}, bf16[4,512,2048]{1,2,0:T(8,128)(2,1)}, s32[]{:T(128)}) while((s32[]{:T(128)}, bf16[4,512,2048]{2,1,0:T(8,128)(2,1)}, s32[4,1]{0,1:T(1,128)S(1)}, bf16[4,512,2048]{1,2,0:T(8,128)(2,1)}, s32[]{:T(128)}) %tuple.314), condition=%wide.while_cond.11, body=%wide.while_body.11.sunk | while | flops 2 | bytes 12583501 | solution.py:33
  1742.4 34.9 %while.41 = (s32[]{:T(128)}, bf16[4,512,2048]{2,1,0:T(8,128)(2,1)}, s32[4,1]{0,1:T(1,128)S(1)}, bf16[4,512,2048]{1,2,0:T(8,128)(2,1)}, s32[]{:T(128)}) while((s32[]{:T(128)}, bf16[4,512,2048]{2,1,0:T(8,128)(2,1)}, s32[4,1]{0,1:T(1,128)S(1)}, bf16[4,512,2048]{1,2,0:T(8,128)(2,1)}, s32[]{:T(128)}) %tuple.315), condition=%wide.while_cond.12, body=%wide.while_body.12.sunk | while | flops 2 | bytes 12583501 | solution.py:33
  1781.1 34.9 %while.42 = (s32[]{:T(128)}, bf16[4,512,2048]{2,1,0:T(8,128)(2,1)}, s32[4,1]{0,1:T(1,128)S(1)}, bf16[4,512,2048]{1,2,0:T(8,128)(2,1)}, s32[]{:T(128)}) while((s32[]{:T(128)}, bf16[4,512,2048]{2,1,0:T(8,128)(2,1)}, s32[4,1]{0,1:T(1,128)S(1)}, bf16[4,512,2048]{1,2,0:T(8,128)(2,1)}, s32[]{:T(128)}) %tuple.316), condition=%wide.while_cond.13, body=%wide.while_body.13.sunk | while | flops 2 | bytes 12583501 | solution.py:33
  1820.1 35.0 %while.43 = (s32[]{:T(128)}, bf16[4,512,2048]{2,1,0:T(8,128)(2,1)}, s32[4,1]{0,1:T(1,128)S(1)}, bf16[4,512,2048]{1,2,0:T(8,128)(2,1)}, s32[]{:T(128)}) while((s32[]{:T(128)}, bf16[4,512,2048]{2,1,0:T(8,128)(2,1)}, s32[4,1]{0,1:T(1,128)S(1)}, bf16[4,512,2048]{1,2,0:T(8,128)(2,1)}, s32[]{:T(128)}) %tuple.317), condition=%wide.while_cond.14, body=%wide.while_body.14.sunk | while | flops 2 | bytes 12583501 | solution.py:33
  1859.1 35.1 %while.44 = (s32[]{:T(128)}, bf16[4,512,2048]{2,1,0:T(8,128)(2,1)}, s32[4,1]{0,1:T(1,128)S(1)}, bf16[4,512,2048]{1,2,0:T(8,128)(2,1)}, s32[]{:T(128)}) while((s32[]{:T(128)}, bf16[4,512,2048]{2,1,0:T(8,128)(2,1)}, s32[4,1]{0,1:T(1,128)S(1)}, bf16[4,512,2048]{1,2,0:T(8,128)(2,1)}, s32[]{:T(128)}) %tuple.318), condition=%wide.while_cond.15, body=%wide.while_body.15.sunk | while | flops 2 | bytes 12583501 | solution.py:33
  2001.3 80.2 %convolution_convert_fusion = bf16[8192,512]{1,0:T(8,128)(2,1)} fusion(bf16[8192,8192]{0,1:T(8,128)(2,1)} %bitcast.8, bf16[512,8192]{1,0:T(8,128)(2,1)} %all-gather.5.cloned.1.call-done), kind=kOutput, calls=%fused_computation.60 | convolution fusion | flops 68723671040 | bytes 150994944 | tf_op jit(solution)/shard_map/dot_general | solution.py:91
  2141.2 45.3 %all-gather.9.cloned.1.call-done = f32[8,32,64,128]{3,2,1,0:T(8,128)} async-done(((f32[2,32,64,128]{3,2,1,0:T(8,128)}), f32[8,32,64,128]{3,2,1,0:T(8,128)}) %all-gather.9.cloned.1.call-update) | async-done | bytes 8388624 | tf_op jit(solution)/shard_map/all_gather | solution.py:45
  2255.2 99.2 %all_to_all.24 = bf16[4,64,64,128]{3,2,1,0:T(8,128)(2,1)} all-to-all(bf16[4,64,64,128]{3,2,1,0:T(8,128)(2,1)} %bitcast.212), channel_id=1, replica_groups=mesh['groups'=2,'seq'=4,'heads'=4] {'heads'}, dimensions={0} | all-to-all | bytes 8388608 | tf_op jit(solution)/shard_map/all_to_all | solution.py:222
  (525 shorter events, 992.4 us)
Async XLA Ops:
  7.2 888.3 %copy-start = (bf16[8192,64]{0,1:T(8,128)(2,1)S(1)}, bf16[8192,64]{0,1:T(8,128)(2,1)}, u32[]{:S(2)}) copy-start(bf16[8192,64]{0,1:T(8,128)(2,1)} %param.19) | copy-start | bytes 3145732
  7.2 873.0 %all-gather.5.cloned.1.call-start = ((), (), s32[]{:S(2)}) async-start(), calls=%async_computation.2 | async-start | bytes 10485760 | tf_op jit(solution)/shard_map/all_gather | solution.py:89
  7.2 721.6 %collective-permute-start = (bf16[8192,2048]{1,0:T(8,128)(2,1)}, bf16[8192,2048]{1,0:T(8,128)(2,1)}, u32[]{:S(2)}, u32[]{:S(2)}) collective-permute-start(bf16[8192,2048]{1,0:T(8,128)(2,1)} %param.17), channel_id=1, source_target_pairs={{0,4},{4,8},{8,12},{12,0},{1,5},{5,9},{9,13},{13,1},{2,6},{6,10},{... | collective-permute-start | bytes 100663304 | tf_op jit(solution)/shard_map/ppermute | solution.py:28
  7.3 930.1 %collective-permute-start.2 = (bf16[8192,2048]{1,0:T(8,128)(2,1)}, bf16[8192,2048]{1,0:T(8,128)(2,1)}, u32[]{:S(2)}, u32[]{:S(2)}) collective-permute-start(bf16[8192,2048]{1,0:T(8,128)(2,1)} %param.17), channel_id=1, source_target_pairs={{4,0},{8,4},{12,8},{0,12},{5,1},{9,5},{13,9},{1,13},{6,2},{10,6},{... | collective-permute-start | bytes 100663304 | tf_op jit(solution)/shard_map/ppermute | solution.py:30
  728.8 362.8 %collective-permute-start.1 = (bf16[8192,2048]{1,0:T(8,128)(2,1)}, bf16[8192,2048]{1,0:T(8,128)(2,1)}, u32[]{:S(2)}, u32[]{:S(2)}) collective-permute-start(bf16[8192,2048]{1,0:T(8,128)(2,1)} %collective-permute-done), channel_id=1, source_target_pairs={{0,4},{4,8},{8,12},{12,0},{1,5},{5,9},{9,13},{13,1},{2,6},{6,10},{... | collective-permute-start | bytes 100663304 | tf_op jit(solution)/shard_map/ppermute | solution.py:28
  728.9 162.4 %copy-start.36 = (f32[4,4096]{1,0:T(4,128)S(1)}, f32[4,4096]{1,0:T(4,128)}, u32[]{:S(2)}) copy-start(f32[4,4096]{1,0:T(4,128)} %param.23) | copy-start | bytes 196612
  728.9 163.1 %copy-start.56 = (f32[64]{0:T(128)S(1)}, f32[64]{0:T(128)}, u32[]{:S(2)}) copy-start(f32[64]{0:T(128)} %param.21) | copy-start | bytes 772
  728.9 166.5 %copy-start.53 = (f32[64]{0:T(128)S(1)}, f32[64]{0:T(128)}, u32[]{:S(2)}) copy-start(f32[64]{0:T(128)} %param.20) | copy-start | bytes 772
  728.9 206.6 %all-gather.7.cloned.1.call-start = ((), (), s32[]{:S(2)}) async-start(), calls=%async_computation.3 | async-start | bytes 2621440 | tf_op jit(solution)/shard_map/all_gather | solution.py:99
  891.2 1295.2 %all-gather.9.cloned.1.call-start = ((), (), s32[]{:S(2)}) async-start(), calls=%async_computation.4 | async-start | bytes 10485760 | tf_op jit(solution)/shard_map/all_gather | solution.py:45
  902.0 277.0 %copy-start.12 = (f32[512,64]{0,1:T(8,128)}, f32[512,64]{0,1:T(8,128)S(1)}, u32[]{:S(2)}) copy-start(f32[512,64]{0,1:T(8,128)S(1)} %compare_select_fusion) | copy-start | bytes 393220
  905.5 273.5 %copy-start.16 = (f32[256,2,32]{0,2,1:T(8,128)}, f32[256,2,32]{0,2,1:T(8,128)S(1)}, u32[]{:S(2)}) copy-start(f32[256,2,32]{0,2,1:T(8,128)S(1)} %bitcast_bitcast_fusion) | copy-start | bytes 196612
  905.6 273.4 %copy-start.19 = (f32[256,2,32]{0,2,1:T(8,128)}, f32[256,2,32]{0,2,1:T(8,128)S(1)}, u32[]{:S(2)}) copy-start(f32[256,2,32]{0,2,1:T(8,128)S(1)} %bitcast_bitcast_fusion.1) | copy-start | bytes 196612
  906.3 272.7 %copy-start.43 = (f32[2,32]{1,0:T(2,128)}, f32[2,32]{1,0:T(2,128)S(1)}, u32[]{:S(2)}) copy-start(f32[2,32]{1,0:T(2,128)S(1)} %get-tuple-element.366) | copy-start | bytes 772
  906.3 272.7 %copy-start.46 = (f32[2,32]{1,0:T(2,128)}, f32[2,32]{1,0:T(2,128)S(1)}, u32[]{:S(2)}) copy-start(f32[2,32]{1,0:T(2,128)S(1)} %get-tuple-element.364) | copy-start | bytes 772
  906.3 272.7 %copy-start.22 = (f32[256,64]{0,1:T(8,128)}, f32[256,64]{0,1:T(8,128)S(1)}, u32[]{:S(2)}) copy-start(f32[256,64]{0,1:T(8,128)S(1)} %get-tuple-element.356) | copy-start | bytes 196612
  906.4 272.7 %copy-start.24 = (f32[256,64]{0,1:T(8,128)}, f32[256,64]{0,1:T(8,128)S(1)}, u32[]{:S(2)}) copy-start(f32[256,64]{0,1:T(8,128)S(1)} %get-tuple-element.357) | copy-start | bytes 196612
  2096.3 5.3 collective-permute-start.3
  2120.2 17.6 copy-start.13
  2120.4 19.6 copy-start.11
  2225.5 14.6 slice-start.3
  2255.2 121.4 %copy-start.41 = (f32[4096]{0:T(1024)S(1)}, f32[4096]{0:T(1024)}, u32[]{:S(2)}) copy-start(f32[4096]{0:T(1024)} %param.27) | copy-start | bytes 49156
  2354.4 59.2 %all-to-all-start.1 = ((bf16[1,256,64,128]{3,2,0,1:T(8,128)(2,1)}), bf16[1,256,64,128]{3,2,0,1:T(8,128)(2,1)}, u32[]{:S(2)}, u32[]{:S(2)}) async-start(bf16[1,256,64,128]{3,2,0,1:T(8,128)(2,1)} %bitcast.211), calls=%async_computation.1 | async-start | bytes 8388608 | tf_op jit(solution)/shard_map/all_to_all | solution.py:221
  2376.6 42.2 %copy-start.1 = (bf16[8192,64]{0,1:T(8,128)(2,1)S(1)}, bf16[8192,64]{0,1:T(8,128)(2,1)}, u32[]{:S(2)}) copy-start(bf16[8192,64]{0,1:T(8,128)(2,1)} %param.19) | copy-start | bytes 3145732
  (48 other events, 338.0 us)
Sparse Core Ops, SparseCore 0:
  729.0 151.1 all-gather.4
  891.4 44.0 all-gather.6
  2127.8 58.5 all-gather.8
